TPU v7x, 32 devices: a whole 2x2x4 slice. The times are simulated.
32 devices in a mesh: band: 4 (over y, core), ma: 8 (over z, x).
Axes of the slice: x: 2, y: 2, z: 4, core: 2. Of those that a mesh axis runs over, the one named last changes fastest.
Arguments:
- sky_maps: bfloat16 [64, 64, 2, 16384], P(None, ('band', 'ma')), may hold values from -6 to 6
- hi_cycles: int32 [64], P(('band', 'ma')), may hold values from 4096 to 8191, as said below
- lo_cycles: int32 [64], P(('band', 'ma')), may hold values from 1024 to 2047, as said below
- azimuth_orders: int32 [128], replicated, may hold values from 0 to 3071, as said below
- legendre_hi: bfloat16 [128, 3072, 64], P(('band', 'ma')), may hold values from -0.75 to 0.75
- legendre_lo: bfloat16 [128, 3072, 64], P(('band', 'ma')), may hold values from -0.109375 to 0.109375
- beam_weights: float32 [3072], replicated, may hold values from 0.05 to 1
Outputs:
- smoothed_maps: float32 [64, 64, 2, 4096], P(None, ('band', 'ma'))
Inputs may be any that keep to these rules, and one draw needn't show every extreme that they name: `hi_cycles`: distinct northern equatorial-belt cycles. `lo_cycles`: distinct northern equatorial-belt cycles. `azimuth_orders`: distinct orders.
All inputs are finite; a program needn't handle non-finite values.
Results may differ from a plain program's by a relative error of at most 0.0038.
Values may be sent and summed in bfloat16 or wider, within the bound.
No kernel may reach another device: no remote copies, remote signals or barrier semaphores. Data moves between devices by JAX's collectives and lax.ppermute only.
A program may use at most 192 MiB of HBM per device.

v0:
```python
import math
import jax
import jax.numpy as jnp
from jax import lax
from jax.sharding import PartitionSpec as P

NSIDE_HI = 4096
NSIDE_LO = 1024
LROWS = 3072
NPIX_HI = 16384
NPIX_LO = 4096
THREE_PASS = lax.Precision.HIGH


def angle_grid(first, second, length):
    product = first[:, None] * second[None, :] % length
    return product.astype(jnp.float32) * (2.0 * math.pi / length)


def cycle_offsets(cycle_ids, side_count):
    return ((cycle_ids - side_count + 1) % 2).astype(jnp.float32)


def per_device(
    sky_maps, hi_cycles, lo_cycles, azimuth_orders, legendre_hi, legendre_lo, beam_weights
):
    map_count = sky_maps.shape[0]
    pair_local = sky_maps.shape[1]
    select_total = azimuth_orders.shape[0]
    owned = legendre_hi.shape[0]
    half_cols = 2 * map_count
    pixels_hi = jnp.arange(NPIX_HI, dtype=jnp.int32)
    angles = angle_grid(pixels_hi, azimuth_orders, NPIX_HI)
    forward_table = jnp.concatenate([jnp.cos(angles), jnp.sin(angles)], axis=1).astype(jnp.bfloat16)
    raw_sums = jnp.dot(
        sky_maps.reshape(-1, NPIX_HI), forward_table, preferred_element_type=jnp.float32
    )
    raw_sums = raw_sums.reshape(map_count, pair_local, 2, 2, select_total)
    real_raw = raw_sums[:, :, :, 0]
    imag_raw = -raw_sums[:, :, :, 1]
    offsets_hi = cycle_offsets(hi_cycles, NSIDE_HI)
    theta_hi = math.pi * offsets_hi[:, None] * azimuth_orders.astype(jnp.float32)[None, :] / NPIX_HI
    cos_hi = jnp.cos(theta_hi)[None, :, None, :]
    sin_hi = jnp.sin(theta_hi)[None, :, None, :]
    scale_hi = 1.0 / math.sqrt(NPIX_HI)
    real_coef = (real_raw * cos_hi + imag_raw * sin_hi) * scale_hi
    imag_coef = (imag_raw * cos_hi - real_raw * sin_hi) * scale_hi
    stacked = jnp.stack([real_coef, imag_coef], axis=3)
    outgoing = (
        jnp.transpose(stacked, (4, 1, 2, 3, 0))
        .reshape(select_total, pair_local, 4 * map_count)
        .astype(jnp.bfloat16)
    )
    owner = lax.axis_index(("band", "ma"))
    own_orders = lax.dynamic_slice_in_dim(azimuth_orders, owner * owned, owned)
    degrees = jnp.arange(LROWS, dtype=jnp.int32)[None, :]
    parity = (degrees + own_orders[:, None]) % 2
    signs_lm = 1.0 - 2.0 * parity.astype(jnp.float32)
    beam_mask = jnp.where(degrees >= own_orders[:, None], beam_weights[None, :], 0.0)
    received = lax.all_to_all(outgoing, ("band", "ma"), split_axis=0, concat_axis=1, tiled=True)
    analysis = jnp.einsum("mlr,mrc->mlc", legendre_hi, received, preferred_element_type=jnp.float32)
    harmonic = analysis[:, :, :half_cols] + signs_lm[..., None] * analysis[:, :, half_cols:]
    weighted = beam_mask[..., None] * harmonic
    paired = jnp.concatenate([weighted, signs_lm[..., None] * weighted], axis=2)
    synthesized = jnp.einsum(
        "mlq,mlc->mqc",
        legendre_lo,
        paired,
        precision=THREE_PASS,
        preferred_element_type=jnp.float32,
    )
    returned = lax.all_to_all(synthesized, ("band", "ma"), split_axis=1, concat_axis=0, tiled=True)
    low_local = returned.shape[1]
    parts_low = returned.reshape(select_total, low_local, 2, 2, map_count)
    real_low = parts_low[:, :, :, 0]
    imag_low = parts_low[:, :, :, 1]
    offsets_lo = cycle_offsets(lo_cycles, NSIDE_LO)
    theta_lo = math.pi * azimuth_orders.astype(jnp.float32)[:, None] * offsets_lo[None, :] / NPIX_LO
    cos_lo = jnp.cos(theta_lo)[:, :, None, None]
    sin_lo = jnp.sin(theta_lo)[:, :, None, None]
    real_rot = real_low * cos_lo - imag_low * sin_lo
    imag_rot = imag_low * cos_lo + real_low * sin_lo
    spectra = jnp.stack([real_rot, imag_rot], axis=0)
    spectra = jnp.transpose(spectra, (4, 2, 3, 0, 1)).reshape(-1, 2 * select_total)
    pixels_lo = jnp.arange(NPIX_LO, dtype=jnp.int32)
    angles_lo = angle_grid(azimuth_orders, pixels_lo, NPIX_LO)
    inverse_table = jnp.concatenate([jnp.cos(angles_lo), -jnp.sin(angles_lo)], axis=0)
    pixels_out = jnp.dot(
        spectra, inverse_table, precision=THREE_PASS, preferred_element_type=jnp.float32
    )
    pixels_out = pixels_out * math.sqrt(2.0 / select_total)
    return pixels_out.reshape(map_count, low_local, 2, NPIX_LO)


def solution(mesh):
    return jax.shard_map(
        per_device,
        mesh=mesh,
        in_specs=(
            P(None, ("band", "ma"), None, None),
            P(("band", "ma")),
            P(("band", "ma")),
            P(),
            P(("band", "ma"), None, None),
            P(("band", "ma"), None, None),
            P(),
        ),
        out_specs=P(None, ("band", "ma"), None, None),
        check_vma=False,
    )
```

profile of v0, /device:TPU:0, one launch (start us, length us, event | category | flops | bytes accessed | tf_op | source)
XLA Modules:
  0.0 116.5 jit_solution(8038480277856101105)
XLA Ops:
  0.0 0.0 copy-start
  0.0 0.0 copy-start.4
  0.0 35.4 %cosine_convert_fusion = (bf16[16384,128]{1,0:T(8,128)(2,1)}, bf16[16384,128]{1,0:T(8,128)(2,1)}) fusion(s32[128]{0:T(128)} %param.10), kind=kLoop, calls=%fused_computation.15 | loop fusion | flops 33554432 | bytes 8389120 | tf_op jit(solution)/shard_map/convert.2
  35.4 0.0 copy-done.4
  35.4 13.1 %reshape.236 = bf16[256,16384]{1,0:T(8,128)(2,1)} reshape(bf16[64,2,2,16384]{3,2,1,0:T(2,128)(2,1)} %param.7) | data formatting | bytes 16777216 | tf_op jit(solution)/shard_map/reshape | solution.py:36
  48.6 0.0 copy-start.5
  48.6 0.0 copy-start.3
  48.6 0.0 copy-start.6
  48.6 8.3 %fusion.25 = f32[256,256]{0,1:T(8,128)S(1)} fusion(bf16[256,16384]{1,0:T(8,128)(2,1)} %reshape.236, bf16[16384,128]{1,0:T(8,128)(2,1)} %get-tuple-element.22, bf16[16384,128]{1,0:T(8,128)(2,1)} %get-tuple-element.21), kind=kOutput, calls=%fused_computation.38 | convolution fusion | flops 2164260864 | bytes 17039360 | tf_op jit(solution)/shard_map/dot_general | solution.py:35
  56.8 0.1 copy.27
  57.0 0.1 reshape.237
  57.1 0.2 fusion.53
  57.3 0.0 copy-done.5
  57.4 0.1 fusion.42
  57.5 0.1 multiply_convert_fusion.1
  57.6 0.8 copy.30
  58.3 7.3 %all-to-all-start = ((bf16[128,2,256]{2,1,0:T(2,128)(2,1)}), bf16[128,2,256]{2,1,0:T(2,128)(2,1)S(1)}, u32[]{:S(2)}, u32[]{:S(2)}) async-start(bf16[128,2,256]{2,1,0:T(2,128)(2,1)} %copy.30), calls=%async_computation | async-start | bytes 262144 | tf_op jit(solution)/shard_map/all_to_all | solution.py:60
  65.7 0.1 dynamic_slice.3
  65.8 0.0 copy-done.3
  65.8 0.1 fusion.38
  65.9 0.0 copy-done.6
  65.9 0.1 fusion.40
  66.1 0.1 copy.36
  66.2 0.1 copy.37
  66.3 7.2 %all-to-all-done = bf16[128,2,256]{2,1,0:T(2,128)(2,1)S(1)} async-done(((bf16[128,2,256]{2,1,0:T(2,128)(2,1)}), bf16[128,2,256]{2,1,0:T(2,128)(2,1)S(1)}, u32[]{:S(2)}, u32[]{:S(2)}) %all-to-all-start) | async-done | bytes 131104 | tf_op jit(solution)/shard_map/all_to_all | solution.py:60
  73.5 0.1 copy.31
  73.6 0.1 all_to_all.27
  73.6 0.0 copy-done
  73.7 1.8 %convolution_bitcast_fusion = f32[4,3072,256]{1,2,0:T(8,128)S(1)} fusion(bf16[4,64,256]{2,1,0:T(8,128)(2,1)S(1)} %all_to_all.27, bf16[4,3072,64]{1,2,0:T(8,128)(2,1)S(1)} %copy-done), kind=kOutput, calls=%fused_computation.19 | convolution fusion | flops 402653184 | bytes 14286848 | tf_op jit(solution)/shard_map/mlr,mrc->mlc/dot_general | solution.py:61
  75.5 0.0 copy-start.2
  75.5 5.6 %broadcast_multiply_fusion = (f32[4,3072,128]{1,2,0:T(8,128)}, f32[4,3072,128]{1,2,0:T(8,128)}) fusion(f32[4,3072]{1,0:T(4,128)S(1)} %get-tuple-element.20, f32[4,3072,256]{1,2,0:T(8,128)S(1)} %convolution_bitcast_fusion, f32[4,3072]{1,0:T(4,128)S(1)} %get-tuple-element.19), kind=kLoop, calls=%fused_computation.30 | loop fusion | flops 6291456 | bytes 25264128 | tf_op jit(solution)/shard_map/mul | solution.py:64
  81.1 0.0 copy-done.2
  81.1 6.9 %fusion.28 = f32[4,64,256]{2,1,0:T(8,128)S(1)} fusion(bf16[4,3072,64]{1,2,0:T(8,128)(2,1)S(1)} %copy-done.2, f32[4,3072,128]{1,2,0:T(8,128)} %get-tuple-element.5, f32[4,3072,128]{1,2,0:T(8,128)} %get-tuple-element.6), kind=kOutput, calls=%fused_computation.39 | convolution fusion | flops 1211105280 | bytes 14417920 | tf_op jit(solution)/shard_map/mlq,mlc->mqc/dot_general | solution.py:65
  88.0 0.9 copy.33
  88.9 2.8 %all-to-all-start.1 = ((f32[4,64,256]{2,0,1:T(4,128)}), f32[4,64,256]{2,0,1:T(4,128)S(1)}, u32[]{:S(2)}, u32[]{:S(2)}) async-start(f32[4,64,256]{2,0,1:T(4,128)} %copy.33), calls=%async_computation.1 | async-start | bytes 524288 | tf_op jit(solution)/shard_map/all_to_all | solution.py:72
  91.7 9.8 %fusion.31 = (f32[128,4096]{1,0:T(8,128)}, f32[128,4096]{1,0:T(8,128)}) fusion(s32[128]{0:T(128)S(1)} %copy-done.4), kind=kLoop, calls=%fused_computation.40 | loop fusion | flops 7864320 | bytes 4194816 | tf_op jit(solution)/shard_map/cos | solution.py:87
  101.4 0.5 all-to-all-done.1
  101.9 0.1 copy.56
  102.1 0.5 reshape.238
  102.5 0.4 fusion.52
  102.9 0.7 multiply_subtract_fusion
  103.7 0.3 maximum_bitcast_fusion
  103.9 0.4 copy.38
  104.3 0.0 copy-start.1
  104.3 6.3 %convolution_multiply_fusion = f32[256,4096]{1,0:T(8,128)} fusion(f32[128,4096]{1,0:T(8,128)} %get-tuple-element.24, f32[128,4096]{1,0:T(8,128)} %get-tuple-element.23, f32[32,8,2,128]{3,2,1,0:T(2,128)S(1)} %bitcast.31), kind=kOutput, calls=%fused_computation.23 | convolution fusion | flops 1612709888 | bytes 8650752 | tf_op jit(solution)/shard_map/dot_general | solution.py:88
  110.6 5.8 %reshape.240 = f32[64,2,2,4096]{3,2,1,0:T(2,128)} reshape(f32[256,4096]{1,0:T(8,128)} %convolution_multiply_fusion) | data formatting | bytes 8388608 | tf_op jit(solution)/shard_map/reshape | solution.py:92
  116.5 0.0 copy-done.1
  (5 shorter events, 0.0 us)
Async XLA Ops:
  0.0 73.6 %copy-start = (bf16[4,3072,64]{1,2,0:T(8,128)(2,1)S(1)}, bf16[4,3072,64]{1,2,0:T(8,128)(2,1)}, u32[]{:S(2)}) copy-start(bf16[4,3072,64]{1,2,0:T(8,128)(2,1)} %param.11) | copy-start | bytes 4718596
  0.0 35.4 %copy-start.4 = (s32[128]{0:T(128)S(1)}, s32[128]{0:T(128)}, u32[]{:S(2)}) copy-start(s32[128]{0:T(128)} %param.10) | copy-start | bytes 1540
  48.6 8.8 %copy-start.5 = (s32[2]{0:T(128)S(1)}, s32[2]{0:T(128)}, u32[]{:S(2)}) copy-start(s32[2]{0:T(128)} %param.8) | copy-start | bytes 28
  48.6 17.2 %copy-start.3 = (f32[3072]{0:T(1024)S(1)}, f32[3072]{0:T(1024)}, u32[]{:S(2)}) copy-start(f32[3072]{0:T(1024)} %param.13) | copy-start | bytes 36868
  48.6 17.4 %copy-start.6 = (s32[2]{0:T(128)S(1)}, s32[2]{0:T(128)}, u32[]{:S(2)}) copy-start(s32[2]{0:T(128)} %param.9) | copy-start | bytes 28
  58.3 15.1 %all-to-all-start = ((bf16[128,2,256]{2,1,0:T(2,128)(2,1)}), bf16[128,2,256]{2,1,0:T(2,128)(2,1)S(1)}, u32[]{:S(2)}, u32[]{:S(2)}) async-start(bf16[128,2,256]{2,1,0:T(2,128)(2,1)} %copy.30), calls=%async_computation | async-start | bytes 262144 | tf_op jit(solution)/shard_map/all_to_all | solution.py:60
  75.5 5.6 %copy-start.2 = (bf16[4,3072,64]{1,2,0:T(8,128)(2,1)S(1)}, bf16[4,3072,64]{1,2,0:T(8,128)(2,1)}, u32[]{:S(2)}) copy-start(bf16[4,3072,64]{1,2,0:T(8,128)(2,1)} %param.12) | copy-start | bytes 4718596
  88.9 13.0 %all-to-all-start.1 = ((f32[4,64,256]{2,0,1:T(4,128)}), f32[4,64,256]{2,0,1:T(4,128)S(1)}, u32[]{:S(2)}, u32[]{:S(2)}) async-start(f32[4,64,256]{2,0,1:T(4,128)} %copy.33), calls=%async_computation.1 | async-start | bytes 524288 | tf_op jit(solution)/shard_map/all_to_all | solution.py:72
  104.3 12.2 %copy-start.1 = (bf16[4,3072,64]{1,2,0:T(8,128)(2,1)S(1)}, bf16[4,3072,64]{1,2,0:T(8,128)(2,1)}, u32[]{:S(2)}) copy-start(bf16[4,3072,64]{1,2,0:T(8,128)(2,1)} %param.11) | copy-start | bytes 4718596
where the time goes:
time: 117 us; the launch traced here: 116 us
  other arithmetic  52.2 us (45%)
  matrix products  23.4 us (20%)
  local copies, waits for them, and re-layouts  22.9 us (20%)
  starting transfers between devices  10.1 us (9%)
  waiting for transfers between devices  7.68 us (7%)
    another operation x2, other arithmetic  35.5 us
    reshape x1, local copies, waits for them, and re-layouts, per_device(): sky_maps.reshape(-1, NPIX_HI)  13.1 us
    cos x1, other arithmetic, per_device(): jnp.cos(angles_lo)  9.79 us
    dot_general x1, matrix products, per_device(): jnp.dot(sky_maps.reshape(-1, NPIX_HI), forward_table, preferred_element_t...  8.27 us
    all_to_all x1, starting transfers between devices, per_device(): lax.all_to_all(outgoing, ('band', 'ma'), split_axis=0, concat_axis=1, til...  7.32 us
    all_to_all x1, waiting for transfers between devices, per_device(): lax.all_to_all(outgoing, ('band', 'ma'), split_axis=0, concat_axis=1, til...  7.21 us
    dot_general x1, matrix products, per_device(): jnp.einsum('mlq,mlc->mqc', legendre_lo, paired, precision=THREE_PASS, pre...  6.94 us
    dot_general x1, matrix products, per_device(): jnp.dot(spectra, inverse_table, precision=THREE_PASS, preferred_element_t...  6.33 us
  transfers between devices with their start and end apart: 2, of which 2 were waited for; matrix products, arithmetic and copies ran while one was open for 9% of the time, Pallas kernels for 0%

commit v1 on v0

--- a/solution.py
+++ b/solution.py
@@ -57,7 +57,10 @@
     parity = (degrees + own_orders[:, None]) % 2
     signs_lm = 1.0 - 2.0 * parity.astype(jnp.float32)
     beam_mask = jnp.where(degrees >= own_orders[:, None], beam_weights[None, :], 0.0)
-    received = lax.all_to_all(outgoing, ("band", "ma"), split_axis=0, concat_axis=1, tiled=True)
+    size = lax.axis_size(("band", "ma"))
+    parts = jnp.stack(jnp.split(outgoing, size, axis=0), axis=0)
+    parts = lax.all_to_all(parts, ("band", "ma"), split_axis=0, concat_axis=0)
+    received = jnp.concatenate(parts, axis=1)
     analysis = jnp.einsum("mlr,mrc->mlc", legendre_hi, received, preferred_element_type=jnp.float32)
     harmonic = analysis[:, :, :half_cols] + signs_lm[..., None] * analysis[:, :, half_cols:]
     weighted = beam_mask[..., None] * harmonic

time: 117 us -> 175 us (1.50)
  local copies, waits for them, and re-layouts: 22.9 us -> 80.4 us
  waiting for transfers between devices: 7.68 us -> 5.05 us
  other arithmetic: 52.2 us -> 54.2 us
    unnamed x14 -> x43, local copies, waits for them, and re-layouts: 0.03 us -> 27.3 us
    another operation x0 -> x33, local copies, waits for them, and re-layouts: none -> 27.1 us  [per_device(): parts = jnp.stack(jnp.split(outgoing, size, axis=0), axis=0)]
    split x0 -> x2, local copies, waits for them, and re-layouts: none -> 3.18 us  [per_device(): parts = jnp.stack(jnp.split(outgoing, size, axis=0), axis=0)]
    all_to_all x1, waiting for transfers between devices: 7.21 us -> 4.39 us  [per_device(): parts = lax.all_to_all(parts, ('band', 'ma'), split_axis=0, concat_axis=0)]
    another operation x3 -> x2, other arithmetic: 35.5 us -> 35.5 us
  transfers between devices with their start and end apart: 2 -> 2, of which waited for: 2 -> 2; matrix products, arithmetic and copies ran while one was open for 9% -> 8% of each run, Pallas kernels for 0% -> 0%
where the time goes in v1:
time: 175 us; the launch traced here: 173 us
  local copies, waits for them, and re-layouts  80.4 us (46%)
  other arithmetic  54.2 us (31%)
  matrix products  23.3 us (13%)
  starting transfers between devices  10.1 us (6%)
  waiting for transfers between devices  5.05 us (3%)
    another operation x2, other arithmetic  35.5 us
    unnamed x43, local copies, waits for them, and re-layouts  27.3 us
    another operation x33, local copies, waits for them, and re-layouts, per_device(): parts = jnp.stack(jnp.split(outgoing, size, axis=0), axis=0)  27.1 us
    reshape x1, local copies, waits for them, and re-layouts, per_device(): sky_maps.reshape(-1, NPIX_HI)  13.1 us
    cos x1, other arithmetic, per_device(): jnp.cos(angles_lo)  9.77 us
    dot_general x1, matrix products, per_device(): jnp.dot(sky_maps.reshape(-1, NPIX_HI), forward_table, preferred_element_t...  8.25 us
    all_to_all x1, starting transfers between devices, per_device(): parts = lax.all_to_all(parts, ('band', 'ma'), split_axis=0, concat_axis=0)  7.51 us
    dot_general x1, matrix products, per_device(): jnp.einsum('mlq,mlc->mqc', legendre_lo, paired, precision=THREE_PASS, pre...  6.95 us
  transfers between devices with their start and end apart: 2, of which 2 were waited for; matrix products, arithmetic and copies ran while one was open for 8% of the time, Pallas kernels for 0%

profile of v1, /device:TPU:0, one launch (start us, length us, event | category | flops | bytes accessed | tf_op | source)
XLA Modules:
  0.0 173.2 jit_solution(471997547188920746)
XLA Ops:
  0.0 35.4 %cosine_convert_fusion = (bf16[16384,128]{1,0:T(8,128)(2,1)}, bf16[16384,128]{1,0:T(8,128)(2,1)}) fusion(s32[128]{0:T(128)} %param.10), kind=kLoop, calls=%fused_computation.15 | loop fusion | flops 33554432 | bytes 8389120 | tf_op jit(solution)/shard_map/convert.2
  35.4 13.1 %reshape.306 = bf16[256,16384]{1,0:T(8,128)(2,1)} reshape(bf16[64,2,2,16384]{3,2,1,0:T(2,128)(2,1)} %param.7) | data formatting | bytes 16777216 | tf_op jit(solution)/shard_map/reshape | solution.py:36
  48.6 8.2 %fusion.25 = f32[256,256]{0,1:T(8,128)S(1)} fusion(bf16[256,16384]{1,0:T(8,128)(2,1)} %reshape.306, bf16[16384,128]{1,0:T(8,128)(2,1)} %get-tuple-element.54, bf16[16384,128]{1,0:T(8,128)(2,1)} %get-tuple-element.53), kind=kOutput, calls=%fused_computation.38 | convolution fusion | flops 2164260864 | bytes 17039360 | tf_op jit(solution)/shard_map/dot_general | solution.py:35
  57.5 1.7 fusion.55
  59.2 1.5 fusion.54
  60.7 1.0 copy.131
  61.7 0.6 constant_dynamic-update-slice_fusion.31
  62.3 1.6 copy.132
  63.9 1.6 copy.133
  65.5 1.6 copy.134
  67.1 1.6 copy.135
  68.7 1.6 copy.136
  70.3 1.6 copy.137
  71.9 1.6 copy.138
  73.5 1.6 copy.139
  75.1 1.6 copy.140
  76.7 1.6 copy.141
  78.3 1.6 copy.142
  79.9 1.6 copy.143
  81.5 1.6 copy.144
  83.1 1.0 copy.145
  84.1 1.0 copy.146
  85.1 1.0 copy.147
  87.9 1.3 constant_dynamic-update-slice_fusion.30
  89.2 1.3 constant_dynamic-update-slice_fusion.29
  90.4 1.3 constant_dynamic-update-slice_fusion.28
  91.7 1.3 constant_dynamic-update-slice_fusion.27
  93.0 1.3 constant_dynamic-update-slice_fusion.26
  94.3 1.3 constant_dynamic-update-slice_fusion.25
  95.5 1.3 constant_dynamic-update-slice_fusion.24
  96.8 1.3 constant_dynamic-update-slice_fusion.23
  98.1 1.3 constant_dynamic-update-slice_fusion.22
  99.4 1.3 constant_dynamic-update-slice_fusion.21
  100.6 1.3 constant_dynamic-update-slice_fusion.20
  101.9 1.3 constant_dynamic-update-slice_fusion.19
  103.2 1.3 constant_dynamic-update-slice_fusion.18
  104.4 0.6 constant_dynamic-update-slice_fusion.17
  105.0 0.6 constant_dynamic-update-slice_fusion.16
  105.6 0.6 constant_dynamic-update-slice_fusion.15
  106.2 0.6 constant_dynamic-update-slice_fusion.14
  107.4 0.6 constant_dynamic-update-slice_fusion.12
  108.0 0.6 constant_dynamic-update-slice_fusion.11
  109.2 0.6 constant_dynamic-update-slice_fusion.9
  109.8 0.6 constant_dynamic-update-slice_fusion.8
  111.0 0.6 constant_dynamic-update-slice_fusion.6
  111.6 0.6 constant_dynamic-update-slice_fusion.5
  112.2 0.6 constant_dynamic-update-slice_fusion.4
  114.0 0.6 constant_dynamic-update-slice_fusion.1
  115.2 7.5 %all-to-all-start = ((bf16[32,4,2,256]{3,2,1,0:T(2,128)(2,1)}), bf16[32,4,2,256]{3,2,1,0:T(2,128)(2,1)S(1)}, u32[]{:S(2)}, u32[]{:S(2)}) async-start(bf16[32,4,2,256]{3,2,1,0:T(2,128)(2,1)} %constant_dynamic-update-slice_fusion), calls=%async_computation | async-start | bytes 262144 | tf_op jit(solution)/shard_map/all_to_all | solution.py:62
  122.7 0.7 broadcast_multiply_fusion.1
  123.3 0.7 dynamic_slice.3
  124.1 0.8 fusion.38
  124.9 0.7 fusion.45
  125.9 4.4 %all-to-all-done = bf16[32,4,2,256]{3,2,1,0:T(2,128)(2,1)S(1)} async-done(((bf16[32,4,2,256]{3,2,1,0:T(2,128)(2,1)}), bf16[32,4,2,256]{3,2,1,0:T(2,128)(2,1)S(1)}, u32[]{:S(2)}, u32[]{:S(2)}) %all-to-all-start) | async-done | bytes 131104 | tf_op jit(solution)/shard_map/all_to_all | solution.py:62
  130.5 1.8 %convolution_bitcast_fusion = f32[4,3072,256]{1,2,0:T(8,128)S(1)} fusion(bf16[4,64,256]{2,1,0:T(8,128)(2,1)S(1)} %reshape.309, bf16[4,3072,64]{1,2,0:T(8,128)(2,1)S(1)} %copy-done), kind=kOutput, calls=%fused_computation.19 | convolution fusion | flops 402653184 | bytes 14286848 | tf_op jit(solution)/shard_map/mlr,mrc->mlc/dot_general | solution.py:64
  132.3 5.5 %broadcast_multiply_fusion = (f32[4,3072,128]{1,2,0:T(8,128)}, f32[4,3072,128]{1,2,0:T(8,128)}) fusion(f32[4,3072]{1,0:T(4,128)S(1)} %get-tuple-element.52, f32[4,3072,256]{1,2,0:T(8,128)S(1)} %convolution_bitcast_fusion, f32[4,3072]{1,0:T(4,128)S(1)} %get-tuple-element.51), kind=kLoop, calls=%fused_computation.30 | loop fusion | flops 6291456 | bytes 25264128 | tf_op jit(solution)/shard_map/mul | solution.py:67
  137.8 7.0 %fusion.28 = f32[4,64,256]{2,1,0:T(8,128)S(1)} fusion(bf16[4,3072,64]{1,2,0:T(8,128)(2,1)S(1)} %copy-done.2, f32[4,3072,128]{1,2,0:T(8,128)} %get-tuple-element.5, f32[4,3072,128]{1,2,0:T(8,128)} %get-tuple-element.6), kind=kOutput, calls=%fused_computation.39 | convolution fusion | flops 1211105280 | bytes 14417920 | tf_op jit(solution)/shard_map/mlq,mlc->mqc/dot_general | solution.py:68
  144.8 0.9 copy.124
  145.7 2.6 %all-to-all-start.1 = ((f32[4,64,256]{2,0,1:T(4,128)}), f32[4,64,256]{2,0,1:T(4,128)S(1)}, u32[]{:S(2)}, u32[]{:S(2)}) async-start(f32[4,64,256]{2,0,1:T(4,128)} %copy.124), calls=%async_computation.1 | async-start | bytes 524288 | tf_op jit(solution)/shard_map/all_to_all | solution.py:75
  148.3 9.8 %fusion.31 = (f32[128,4096]{1,0:T(8,128)}, f32[128,4096]{1,0:T(8,128)}) fusion(s32[128]{0:T(128)S(1)} %copy-done.4), kind=kLoop, calls=%fused_computation.40 | loop fusion | flops 7864320 | bytes 4194816 | tf_op jit(solution)/shard_map/cos | solution.py:90
  158.0 0.7 all-to-all-done.1
  159.7 0.7 multiply_subtract_fusion
  161.1 6.3 %convolution_multiply_fusion = f32[256,4096]{1,0:T(8,128)} fusion(f32[128,4096]{1,0:T(8,128)} %get-tuple-element.56, f32[128,4096]{1,0:T(8,128)} %get-tuple-element.55, f32[32,8,2,128]{3,2,1,0:T(2,128)S(1)} %bitcast.60), kind=kOutput, calls=%fused_computation.23 | convolution fusion | flops 1612709888 | bytes 8650752 | tf_op jit(solution)/shard_map/dot_general | solution.py:91
  167.4 5.8 %reshape.312 = f32[64,2,2,4096]{3,2,1,0:T(2,128)} reshape(f32[256,4096]{1,0:T(8,128)} %convolution_multiply_fusion) | data formatting | bytes 8388608 | tf_op jit(solution)/shard_map/reshape | solution.py:95
  (51 shorter events, 8.1 us)
Async XLA Ops:
  0.0 130.5 %copy-start = (bf16[4,3072,64]{1,2,0:T(8,128)(2,1)S(1)}, bf16[4,3072,64]{1,2,0:T(8,128)(2,1)}, u32[]{:S(2)}) copy-start(bf16[4,3072,64]{1,2,0:T(8,128)(2,1)} %param.11) | copy-start | bytes 4718596
  0.0 35.4 %copy-start.3 = (s32[128]{0:T(128)S(1)}, s32[128]{0:T(128)}, u32[]{:S(2)}) copy-start(s32[128]{0:T(128)} %param.10) | copy-start | bytes 1540
  48.6 8.8 %copy-start.5 = (s32[2]{0:T(128)S(1)}, s32[2]{0:T(128)}, u32[]{:S(2)}) copy-start(s32[2]{0:T(128)} %param.8) | copy-start | bytes 28
  115.2 15.1 %all-to-all-start = ((bf16[32,4,2,256]{3,2,1,0:T(2,128)(2,1)}), bf16[32,4,2,256]{3,2,1,0:T(2,128)(2,1)S(1)}, u32[]{:S(2)}, u32[]{:S(2)}) async-start(bf16[32,4,2,256]{3,2,1,0:T(2,128)(2,1)} %constant_dynamic-update-slice_fusion), calls=%async_computation | async-start | bytes 262144 | tf_op jit(solution)/shard_map/all_to_all | solution.py:62
  132.3 5.5 %copy-start.2 = (bf16[4,3072,64]{1,2,0:T(8,128)(2,1)S(1)}, bf16[4,3072,64]{1,2,0:T(8,128)(2,1)}, u32[]{:S(2)}) copy-start(bf16[4,3072,64]{1,2,0:T(8,128)(2,1)} %param.12) | copy-start | bytes 4718596
  137.8 10.4 %copy-start.4 = (s32[128]{0:T(128)S(1)}, s32[128]{0:T(128)}, u32[]{:S(2)}) copy-start(s32[128]{0:T(128)} %param.10) | copy-start | bytes 1540
  145.7 13.0 %all-to-all-start.1 = ((f32[4,64,256]{2,0,1:T(4,128)}), f32[4,64,256]{2,0,1:T(4,128)S(1)}, u32[]{:S(2)}, u32[]{:S(2)}) async-start(f32[4,64,256]{2,0,1:T(4,128)} %copy.124), calls=%async_computation.1 | async-start | bytes 524288 | tf_op jit(solution)/shard_map/all_to_all | solution.py:75
  161.1 12.1 %copy-start.1 = (bf16[4,3072,64]{1,2,0:T(8,128)(2,1)S(1)}, bf16[4,3072,64]{1,2,0:T(8,128)(2,1)}, u32[]{:S(2)}) copy-start(bf16[4,3072,64]{1,2,0:T(8,128)(2,1)} %param.11) | copy-start | bytes 4718596
